TPU v7x, 256 devices: a whole 4x4x8 slice. The times are simulated.
256 devices in a mesh: dp: 4 (over x), expert: 64 (over z, y, core).
Axes of the slice: x: 4, y: 4, z: 8, core: 2. Of those that a mesh axis runs over, the one named last changes fastest.
Arguments:
- cell_table: bfloat16 [524288, 256], P(('dp', 'expert')), may hold values from -6 to 6
- sample_index: int32 [262144], P(('dp', 'expert')), may hold values from 0 to 2047
- region: int32 [262144, 1], P(('dp', 'expert')), may hold values from 0 to 63; in each aligned block of 1024 rows (0 to 1023, 1024 to 2047, ...) at most 32 rows name the same one
- targets: bfloat16 [262144, 256], P(('dp', 'expert')), may hold values from -6 to 6
- trunk_weight: bfloat16 [256, 256], replicated, may hold values from -0.375 to 0.375
- expert_params: float32 [64, 2, 256, 2048], P('expert', None, None, 'dp'), may hold values from -0.375 to 0.375
- first_moment: float32 [64, 2, 256, 2048], P('expert', None, None, 'dp'), may hold values from -4 to 4
- second_moment: float32 [64, 2, 256, 2048], P('expert', None, None, 'dp'), may hold values from 0.05 to 1
Outputs:
- trunk_grad: float32 [256, 256], replicated
- row_loss: float32 [262144], P(('dp', 'expert'))
- new_params: float32 [64, 2, 256, 2048], P('expert', None, None, 'dp')
- new_first: float32 [64, 2, 256, 2048], P('expert', None, None, 'dp')
- new_second: float32 [64, 2, 256, 2048], P('expert', None, None, 'dp')
Inputs may be any that keep to these rules, and one draw needn't show every extreme that they name: In the 1024 rows of one device no region is named more than 32 times; some region exactly 32 times. `sample_index`: indexes the rows of the same device's block of cell_table.
All inputs are finite; a program needn't handle non-finite values.
Results may differ from a plain program's by a relative error of at most 0.0044.
Values may be sent and summed in bfloat16 or wider, within the bound.
A program may use at most 128 MiB of HBM per device.

v0:
```python
import jax
import jax.numpy as jnp
from jax import lax
from jax.sharding import PartitionSpec as P

loss_scale = 1.0 / 32.0
beta_one = 0.9
beta_two = 0.999
learn_rate = 0.05
adam_eps = 1e-08
adam_step = 10


def silu_slope(values):
    sigma = jax.nn.sigmoid(values)
    return sigma * (1.0 + values * (1.0 - sigma))


def adam_update(params, first, second, grads):
    first_new = beta_one * first + (1.0 - beta_one) * grads
    second_new = beta_two * second + (1.0 - beta_two) * grads * grads
    first_hat = first_new / (1.0 - beta_one**adam_step)
    second_hat = second_new / (1.0 - beta_two**adam_step)
    return (
        params - learn_rate * first_hat / (jnp.sqrt(second_hat) + adam_eps),
        first_new,
        second_new,
    )


def on_device(
    cell_table,
    sample_index,
    region,
    targets,
    trunk_weight,
    expert_params,
    first_moment,
    second_moment,
):
    rows = sample_index.shape[0]
    width = cell_table.shape[1]
    experts = lax.axis_size("expert")
    capacity = 2 * rows // experts
    features = jnp.take(cell_table, sample_index, axis=0)
    routed = region[:, 0]
    onehot = (routed[:, None] == jnp.arange(experts, dtype=jnp.int32)[None, :]).astype(jnp.int32)
    slots = jnp.sum(jnp.cumsum(onehot, axis=0) * onehot, axis=1) - 1
    places = routed * capacity + slots
    gathered = lax.all_gather(expert_params.astype(jnp.bfloat16), "dp", axis=3, tiled=True)
    w_up = gathered[0, 0]
    w_down = gathered[0, 1]
    payload = jnp.concatenate([features, targets], axis=1)
    packed = jnp.zeros((experts * capacity, 2 * width), jnp.bfloat16).at[places].set(payload)
    arrived = lax.all_to_all(
        packed.reshape(experts, capacity, 2 * width),
        "expert",
        split_axis=0,
        concat_axis=0,
        tiled=True,
    ).reshape(-1, 2 * width)
    feats = arrived[:, :width]
    there = arrived[:, width:]
    trunk_pre = jnp.dot(feats, trunk_weight, preferred_element_type=jnp.float32)
    trunk_out = (feats.astype(jnp.float32) + jax.nn.silu(trunk_pre)).astype(jnp.bfloat16)
    up_pre = jnp.dot(trunk_out, w_up, preferred_element_type=jnp.float32)
    hidden = jax.nn.silu(up_pre).astype(jnp.bfloat16)
    predicted = lax.dot_general(
        hidden, w_down, (((1,), (1,)), ((), ())), preferred_element_type=jnp.float32
    )
    errors = predicted - there.astype(jnp.float32)
    losses = jnp.sum(errors * errors, axis=1) * (0.5 * loss_scale)
    scaled = (errors * loss_scale).astype(jnp.bfloat16)
    back = lax.all_to_all(
        losses.reshape(experts, capacity), "expert", split_axis=0, concat_axis=0, tiled=True
    )
    row_loss = back.reshape(-1)[places]
    grad_down = lax.dot_general(
        scaled, hidden, (((0,), (0,)), ((), ())), preferred_element_type=jnp.float32
    )
    hidden_grad = jnp.dot(scaled, w_down, preferred_element_type=jnp.float32)
    pre_grad = (hidden_grad * silu_slope(up_pre)).astype(jnp.bfloat16)
    grad_up = lax.dot_general(
        trunk_out, pre_grad, (((0,), (0,)), ((), ())), preferred_element_type=jnp.float32
    )
    row_grad = lax.dot_general(
        pre_grad, w_up, (((1,), (1,)), ((), ())), preferred_element_type=jnp.float32
    ).astype(jnp.bfloat16)
    trunk_slope = (row_grad.astype(jnp.float32) * silu_slope(trunk_pre)).astype(jnp.bfloat16)
    trunk_local = lax.dot_general(
        feats, trunk_slope, (((0,), (0,)), ((), ())), preferred_element_type=jnp.float32
    )
    trunk_grad = lax.psum(trunk_local, ("dp", "expert"))
    grads = jnp.stack([grad_up, grad_down])[None]
    grad_shard = lax.psum_scatter(grads, "dp", scatter_dimension=3, tiled=True)
    new_params, new_first, new_second = adam_update(
        expert_params, first_moment, second_moment, grad_shard
    )
    return (trunk_grad, row_loss, new_params, new_first, new_second)


def solution(mesh):
    placed = (
        P(("dp", "expert"), None),
        P(("dp", "expert")),
        P(("dp", "expert"), None),
        P(("dp", "expert"), None),
        P(),
        P("expert", None, None, "dp"),
        P("expert", None, None, "dp"),
        P("expert", None, None, "dp"),
    )
    return jax.shard_map(
        on_device,
        mesh=mesh,
        in_specs=placed,
        out_specs=(
            P(),
            P(("dp", "expert")),
            P("expert", None, None, "dp"),
            P("expert", None, None, "dp"),
            P("expert", None, None, "dp"),
        ),
        check_vma=False,
    )
```

profile of v0, /device:TPU:2, one launch (start us, length us, event | category | flops | bytes accessed | tf_op | source)
XLA Modules:
  0.0 451.5 jit_solution(14048339895175946293)
XLA Ops:
  7.2 0.8 fusion.17
  8.0 0.7 compare_and_fusion
  8.7 0.7 fusion.16
  9.4 18.0 %reduce-window.6 = s32[64,8,128]{2,1,0:T(8,128)S(1)} reduce-window(s32[64,8,128]{2,1,0:T(8,128)S(1)} %fusion.16, s32[]{:T(128)} %constant.20.clone.1), window={size=1x1x128 pad=0_0x0_0x127_0}, to_apply=%region_0.1 | reduce-window | flops 8323072 | bytes 524292 | tf_op jit(solution)/shard_map/reduce-window
  27.4 0.1 slice.28
  27.5 0.1 copy.17
  27.8 0.1 broadcast_add_fusion
  28.1 3.9 gather_fusion
  32.0 0.2 broadcast_select_fusion
  32.2 6.7 %scatter_custom_fusion = bf16[2048,512]{1,0:T(8,128)(2,1)} fusion(s32[1024]{0:T(1024)S(1)} %bitcast.54, bf16[1024,256]{1,0:T(8,128)(2,1)S(1)} %copy-done.4, bf16[]{:T(256)} %constant.67, bf16[1024,256]{1,0:T(8,128)(2,1)S(1)} %broadcast_select_fusion, bf16[]{:T(256)} %constant.18.clone.1), kind=kCustom, calls=%fused_computation.22 | custom fusion | flops 2097152 | bytes 3145732 | tf_op jit(solution)/shard_map/scatter | solution.py:54
  38.9 12.1 %all-to-all-start = ((bf16[64,32,512]{2,1,0:T(8,128)(2,1)}), bf16[64,32,512]{2,1,0:T(8,128)(2,1)S(1)}, u32[]{:S(2)}, u32[]{:S(2)}) async-start(bf16[64,32,512]{2,1,0:T(8,128)(2,1)} %bitcast.6), calls=%async_computation | async-start | bytes 4194304 | tf_op jit(solution)/shard_map/all_to_all | solution.py:55
  51.1 2.1 convert_element_type.38
  53.2 0.2 reduce-scatter.2.cloned.1.call-start
  53.5 48.9 %all-to-all-done = bf16[64,32,512]{2,1,0:T(8,128)(2,1)S(1)} async-done(((bf16[64,32,512]{2,1,0:T(8,128)(2,1)}), bf16[64,32,512]{2,1,0:T(8,128)(2,1)S(1)}, u32[]{:S(2)}, u32[]{:S(2)}) %all-to-all-start) | async-done | bytes 2097184 | tf_op jit(solution)/shard_map/all_to_all | solution.py:55
  102.4 1.7 fusion.12
  104.2 10.1 %multiply_convert_fusion.1 = (bf16[2048,2048]{1,0:T(8,128)(2,1)S(1)}, f32[2048,2048]{1,0:T(8,128)}) fusion(bf16[1,2,256,2048]{3,2,1,0:T(8,128)(2,1)} %all-gather.2.cloned.1.call-done, f32[2048,256]{1,0:T(8,128)} %fusion.12, bf16[2048,512]{1,0:T(8,128)(2,1)S(1)} %bitcast.46), kind=kOutput, calls=%fused_computation.4 | convolution fusion | flops 2172125184 | bytes 29360128 | tf_op jit(solution)/shard_map/dot_general | solution.py:66
  114.3 2.6 multiply_reduce_fusion
  116.9 2.3 convolution_bitcast_fusion
  119.3 13.3 %multiply_convert_fusion = bf16[2048,2048]{1,0:T(8,128)(2,1)} fusion(f32[2048,2048]{1,0:T(8,128)} %get-tuple-element.9, bf16[1,2,256,2048]{3,2,1,0:T(8,128)(2,1)S(1)} %copy-done.7, f32[2048,256]{1,0:T(8,128)S(1)} %get-tuple-element.11), kind=kOutput, calls=%fused_computation.3 | convolution fusion | flops 2186280960 | bytes 28311552 | tf_op jit(solution)/shard_map/dot_general | solution.py:81
  132.6 5.8 %convolution_bitcast_fusion.1 = f32[1,256,2048]{2,1,0:T(8,128)S(1)} fusion(bf16[2048,2048]{1,0:T(8,128)(2,1)} %multiply_convert_fusion, f32[2048,256]{1,0:T(8,128)S(1)} %copy-done.2, bf16[2048,512]{1,0:T(8,128)(2,1)S(1)} %bitcast.48), kind=kOutput, calls=%fused_computation.8 | convolution fusion | flops 2151153664 | bytes 13631488 | tf_op jit(solution)/shard_map/dot_general | solution.py:83
  138.4 2.2 maximum_bitcast_fusion
  140.7 0.7 mul.111
  141.3 5.6 %all-to-all-start.1 = ((f32[64,1,32]{2,1,0:T(1,128)}), f32[64,1,32]{2,1,0:T(1,128)S(1)}, u32[]{:S(2)}, u32[]{:S(2)}) async-start(f32[64,1,32]{2,1,0:T(1,128)} %bitcast.10), calls=%async_computation.1 | async-start | bytes 65536 | tf_op jit(solution)/shard_map/all_to_all | solution.py:74
  147.0 9.0 %fusion.9 = f32[256,256]{1,0:T(8,128)} fusion(bf16[2048,2048]{1,0:T(8,128)(2,1)} %multiply_convert_fusion, f32[2048,256]{1,0:T(8,128)} %fusion.12, bf16[1,2,256,2048]{3,2,1,0:T(8,128)(2,1)} %all-gather.2.cloned.1.call-done, bf16[2048,512]{1,0:T(8,128)(2,1)S(1)} %bitcast.49), kind=kOutput, calls=%fused_computation.29 | convolution fusion | flops 2421686272 | bytes 12845056 | tf_op jit(solution)/shard_map/dot_general | solution.py:90
  156.0 0.5 all-to-all-done.1
  156.4 0.5 broadcast.88
  157.0 0.7 reduce.3
  157.8 10.5 %gather_fusion.1 = f32[1024]{0:T(1024)} fusion(f32[2048]{0:T(1024)S(1)} %reshape.69, s32[1024]{0:T(1024)S(1)} %broadcast_clamp_fusion), kind=kCustom, calls=%fused_computation.1 | custom fusion | bytes 12288 | tf_op jit(solution)/shard_map/gather | solution.py:77
  168.3 16.8 %reduce-scatter.2.cloned.1.call-done = f32[1,2,256,512]{3,2,1,0:T(8,128)} async-done(((f32[1,2,256,2048]{3,2,1,0:T(8,128)}), f32[1,2,256,512]{3,2,1,0:T(8,128)}) %reduce-scatter.2.cloned.1.call-update) | async-done | bytes 1048592 | tf_op jit(solution)/shard_map/reduce_scatter | solution.py:95
  185.1 3.7 divide_subtract_fusion
  188.8 254.6 %all-reduce.2.cloned.1.call-done = f32[256,256]{1,0:T(8,128)} async-done(((f32[256,256]{1,0:T(8,128)}), f32[256,256]{1,0:T(8,128)}) %all-reduce.2.cloned.1.call-update) | async-done | bytes 262160 | tf_op jit(solution)/shard_map/psum | solution.py:93
  443.3 1.7 copy.25
  (31 shorter events, 0.5 us)
Async XLA Ops:
  7.2 20.9 %copy-start = (bf16[2048,256]{1,0:T(8,128)(2,1)S(1)}, bf16[2048,256]{1,0:T(8,128)(2,1)}, u32[]{:S(2)}) copy-start(bf16[2048,256]{1,0:T(8,128)(2,1)} %param.8) | copy-start | bytes 3145732
  7.2 20.8 %copy-start.6 = (s32[1024,1]{0,1:T(1,128)S(1)}, s32[1024,1]{0,1:T(1,128)}, u32[]{:S(2)}) copy-start(s32[1024,1]{0,1:T(1,128)} %param.10) | copy-start | bytes 12292
  28.1 4.2 copy-start.4
  38.9 63.5 %all-to-all-start = ((bf16[64,32,512]{2,1,0:T(8,128)(2,1)}), bf16[64,32,512]{2,1,0:T(8,128)(2,1)S(1)}, u32[]{:S(2)}, u32[]{:S(2)}) async-start(bf16[64,32,512]{2,1,0:T(8,128)(2,1)} %bitcast.6), calls=%async_computation | async-start | bytes 4194304 | tf_op jit(solution)/shard_map/all_to_all | solution.py:55
  51.0 51.4 %copy-start.5 = (bf16[256,256]{1,0:T(8,128)(2,1)S(1)}, bf16[256,256]{1,0:T(8,128)(2,1)}, u32[]{:S(2)}) copy-start(bf16[256,256]{1,0:T(8,128)(2,1)} %param.12) | copy-start | bytes 393220
  51.1 53.1 %all-gather.2.cloned.1.call-start = ((), (), s32[]{:S(2)}) async-start(), calls=%async_computation.3 | async-start | bytes 2621440 | tf_op jit(solution)/shard_map/all_gather | solution.py:50
  53.2 131.8 %reduce-scatter.2.cloned.1.call-start = ((), (), s32[]{:S(2)}) async-start(), calls=%async_computation.5 | async-start | bytes 5242880 | tf_op jit(solution)/shard_map/reduce_scatter | solution.py:95
  104.1 10.1 %copy-start.7 = (bf16[1,2,256,2048]{3,2,1,0:T(8,128)(2,1)S(1)}, bf16[1,2,256,2048]{3,2,1,0:T(8,128)(2,1)}, u32[]{:S(2)}) copy-start(bf16[1,2,256,2048]{3,2,1,0:T(8,128)(2,1)} %all-gather.2.cloned.1.call-done) | copy-start | bytes 6291460
  119.3 13.3 %copy-start.2 = (f32[2048,256]{1,0:T(8,128)S(1)}, f32[2048,256]{1,0:T(8,128)}, u32[]{:S(2)}) copy-start(f32[2048,256]{1,0:T(8,128)} %fusion.12) | copy-start | bytes 6291460
  141.3 15.1 %all-to-all-start.1 = ((f32[64,1,32]{2,1,0:T(1,128)}), f32[64,1,32]{2,1,0:T(1,128)S(1)}, u32[]{:S(2)}, u32[]{:S(2)}) async-start(f32[64,1,32]{2,1,0:T(1,128)} %bitcast.10), calls=%async_computation.1 | async-start | bytes 65536 | tf_op jit(solution)/shard_map/all_to_all | solution.py:74
  146.9 296.4 %all-reduce.2.cloned.1.call-start = ((), (), s32[]{:S(2)}) async-start(), calls=%async_computation.4 | async-start | bytes 524288 | tf_op jit(solution)/shard_map/psum | solution.py:93
  157.8 27.3 %copy-start.1 = (f32[1,2,256,512]{3,2,1,0:T(8,128)S(1)}, f32[1,2,256,512]{3,2,1,0:T(8,128)}, u32[]{:S(2)}) copy-start(f32[1,2,256,512]{3,2,1,0:T(8,128)} %param.13) | copy-start | bytes 3145732
  157.8 27.3 %copy-start.3 = (f32[1,2,256,512]{3,2,1,0:T(8,128)S(1)}, f32[1,2,256,512]{3,2,1,0:T(8,128)}, u32[]{:S(2)}) copy-start(f32[1,2,256,512]{3,2,1,0:T(8,128)} %param.14) | copy-start | bytes 3145732
Sparse Core Ops, SparseCore 0:
  54.3 33.5 all-gather.1
  140.7 44.3 reduce-scatter.1
  192.0 251.2 all-reduce.1
where the time goes:
time: 452 us
  waiting for transfers between devices  321 us (71%)
  matrix products  44.9 us (10%)
  other arithmetic  36.1 us (8%)
  starting transfers between devices  18 us (4%)
  local copies, waits for them, and re-layouts  17.8 us (4%)
  between operations  13.9 us (3%)
    psum x1, waiting for transfers between devices, on_device(): trunk_grad = lax.psum(trunk_local, ('dp', 'expert'))  255 us
    all_to_all x1, waiting for transfers between devices, on_device(): lax.all_to_all(packed.reshape(experts, capacity, 2 * width), 'expert', sp...  48.9 us
    another operation x3, other arithmetic  18.2 us
    reduce_scatter x1, waiting for transfers between devices, on_device(): grad_shard = lax.psum_scatter(grads, 'dp', scatter_dimension=3, tiled=True)  16.8 us
    dot_general x1, matrix products, on_device(): hidden_grad = jnp.dot(scaled, w_down, preferred_element_type=jnp.float32)  13.3 us
    all_to_all x1, starting transfers between devices, on_device(): lax.all_to_all(packed.reshape(experts, capacity, 2 * width), 'expert', sp...  12.1 us
    gather x1, local copies, waits for them, and re-layouts, on_device(): row_loss = back.reshape(-1)[places]  10.5 us
    dot_general x1, matrix products, on_device(): up_pre = jnp.dot(trunk_out, w_up, preferred_element_type=jnp.float32)  10.1 us
  transfers between devices with their start and end apart: 5, of which 4 were waited for; matrix products, arithmetic and copies ran while one was open for 6% of the time, Pallas kernels for 0%

commit v1 on v0

--- a/solution.py
+++ b/solution.py
@@ -90,7 +90,9 @@
     trunk_local = lax.dot_general(
         feats, trunk_slope, (((0,), (0,)), ((), ())), preferred_element_type=jnp.float32
     )
-    trunk_grad = lax.psum(trunk_local, ("dp", "expert"))
+    trunk_grad = trunk_local
+    for over in ("expert", "dp"):
+        trunk_grad = lax.psum(trunk_grad, over)
     grads = jnp.stack([grad_up, grad_down])[None]
     grad_shard = lax.psum_scatter(grads, "dp", scatter_dimension=3, tiled=True)
     new_params, new_first, new_second = adam_update(

time: 452 us -> 427 us (0.945)
  waiting for transfers between devices: 321 us -> 292 us
    psum x1 -> x2, waiting for transfers between devices: 255 us -> 184 us  [on_device(): trunk_grad = lax.psum(trunk_grad, over)]
    reduce_scatter x1, waiting for transfers between devices: 16.8 us -> 49.5 us  [on_device(): grad_shard = lax.psum_scatter(grads, 'dp', scatter_dimension=3, tiled=True)]
    all_to_all x1, waiting for transfers between devices: 0.48 us -> 9.45 us  [on_device(): lax.all_to_all(losses.reshape(experts, capacity), 'expert', split_axis=0,...]
  transfers between devices with their start and end apart: 5 -> 6, of which waited for: 4 -> 5; matrix products, arithmetic and copies ran while one was open for 6% -> 6% of each run, Pallas kernels for 0% -> 0%
where the time goes in v1:
time: 427 us; the launch traced here: 426 us
  waiting for transfers between devices  292 us (68%)
  matrix products  46 us (11%)
  other arithmetic  37.8 us (9%)
  local copies, waits for them, and re-layouts  17.8 us (4%)
  starting transfers between devices  17.8 us (4%)
  between operations  14 us (3%)
    psum x2, waiting for transfers between devices, on_device(): trunk_grad = lax.psum(trunk_grad, over)  184 us
    reduce_scatter x1, waiting for transfers between devices, on_device(): grad_shard = lax.psum_scatter(grads, 'dp', scatter_dimension=3, tiled=True)  49.5 us
    all_to_all x1, waiting for transfers between devices, on_device(): lax.all_to_all(packed.reshape(experts, capacity, 2 * width), 'expert', sp...  48.9 us
    another operation x3, other arithmetic  18.2 us
    dot_general x1, matrix products, on_device(): hidden_grad = jnp.dot(scaled, w_down, preferred_element_type=jnp.float32)  13.3 us
    all_to_all x1, starting transfers between devices, on_device(): lax.all_to_all(packed.reshape(experts, capacity, 2 * width), 'expert', sp...  12.1 us
    gather x1, local copies, waits for them, and re-layouts, on_device(): row_loss = back.reshape(-1)[places]  10.5 us
    dot_general x1, matrix products, on_device(): up_pre = jnp.dot(trunk_out, w_up, preferred_element_type=jnp.float32)  10.2 us
  transfers between devices with their start and end apart: 6, of which 5 were waited for; matrix products, arithmetic and copies ran while one was open for 6% of the time, Pallas kernels for 0%

profile of v1, /device:TPU:2, one launch (start us, length us, event | category | flops | bytes accessed | tf_op | source)
XLA Modules:
  0.0 425.5 jit_solution(17517683685203440981)
XLA Ops:
  7.2 0.8 fusion.17
  8.0 0.7 compare_and_fusion
  8.7 0.7 fusion.16
  9.4 18.0 %reduce-window.6 = s32[64,8,128]{2,1,0:T(8,128)S(1)} reduce-window(s32[64,8,128]{2,1,0:T(8,128)S(1)} %fusion.16, s32[]{:T(128)} %constant.20.clone.1), window={size=1x1x128 pad=0_0x0_0x127_0}, to_apply=%region_0.1 | reduce-window | flops 8323072 | bytes 524292 | tf_op jit(solution)/shard_map/reduce-window
  27.5 0.1 copy.17
  27.8 0.1 broadcast_add_fusion
  28.1 3.9 gather_fusion
  32.0 0.2 broadcast_select_fusion
  32.2 6.7 %scatter_custom_fusion = bf16[2048,512]{1,0:T(8,128)(2,1)} fusion(s32[1024]{0:T(1024)S(1)} %bitcast.54, bf16[1024,256]{1,0:T(8,128)(2,1)S(1)} %copy-done.6, bf16[]{:T(256)} %constant.67, bf16[1024,256]{1,0:T(8,128)(2,1)S(1)} %broadcast_select_fusion, bf16[]{:T(256)} %constant.18.clone.1), kind=kCustom, calls=%fused_computation.22 | custom fusion | flops 2097152 | bytes 3145732 | tf_op jit(solution)/shard_map/scatter | solution.py:54
  38.9 12.1 %all-to-all-start = ((bf16[64,32,512]{2,1,0:T(8,128)(2,1)}), bf16[64,32,512]{2,1,0:T(8,128)(2,1)S(1)}, u32[]{:S(2)}, u32[]{:S(2)}) async-start(bf16[64,32,512]{2,1,0:T(8,128)(2,1)} %bitcast.6), calls=%async_computation | async-start | bytes 4194304 | tf_op jit(solution)/shard_map/all_to_all | solution.py:55
  51.1 2.1 convert_element_type.38
  53.2 0.2 all-reduce.3.cloned.1.call-start
  53.5 48.9 %all-to-all-done = bf16[64,32,512]{2,1,0:T(8,128)(2,1)S(1)} async-done(((bf16[64,32,512]{2,1,0:T(8,128)(2,1)}), bf16[64,32,512]{2,1,0:T(8,128)(2,1)S(1)}, u32[]{:S(2)}, u32[]{:S(2)}) %all-to-all-start) | async-done | bytes 2097184 | tf_op jit(solution)/shard_map/all_to_all | solution.py:55
  102.4 2.0 fusion.12
  104.4 10.2 %multiply_convert_fusion.1 = (bf16[2048,2048]{1,0:T(8,128)(2,1)S(1)}, f32[2048,2048]{1,0:T(8,128)}) fusion(bf16[1,2,256,2048]{3,2,1,0:T(8,128)(2,1)} %all-gather.2.cloned.1.call-done, f32[2048,256]{1,0:T(8,128)} %fusion.12, bf16[2048,512]{1,0:T(8,128)(2,1)S(1)} %bitcast.46), kind=kOutput, calls=%fused_computation.4 | convolution fusion | flops 2172125184 | bytes 29360128 | tf_op jit(solution)/shard_map/dot_general | solution.py:66
  114.6 2.6 multiply_reduce_fusion
  117.2 2.3 convolution_bitcast_fusion
  119.6 13.3 %multiply_convert_fusion = bf16[2048,2048]{1,0:T(8,128)(2,1)} fusion(f32[2048,2048]{1,0:T(8,128)} %get-tuple-element.9, bf16[1,2,256,2048]{3,2,1,0:T(8,128)(2,1)S(1)} %copy-done.9, f32[2048,256]{1,0:T(8,128)S(1)} %get-tuple-element.11), kind=kOutput, calls=%fused_computation.3 | convolution fusion | flops 2186280960 | bytes 28311552 | tf_op jit(solution)/shard_map/dot_general | solution.py:81
  132.9 7.1 %convolution_bitcast_fusion.1 = f32[1,256,2048]{2,1,0:T(8,128)} fusion(bf16[2048,2048]{1,0:T(8,128)(2,1)} %multiply_convert_fusion, f32[2048,256]{1,0:T(8,128)S(1)} %copy-done.4, bf16[2048,512]{1,0:T(8,128)(2,1)S(1)} %bitcast.49), kind=kOutput, calls=%fused_computation.8 | convolution fusion | flops 2151153664 | bytes 13631488 | tf_op jit(solution)/shard_map/dot_general | solution.py:83
  140.0 8.5 %fusion.9 = f32[256,256]{1,0:T(8,128)} fusion(bf16[2048,2048]{1,0:T(8,128)(2,1)} %multiply_convert_fusion, f32[2048,256]{1,0:T(8,128)} %fusion.12, bf16[1,2,256,2048]{3,2,1,0:T(8,128)(2,1)} %all-gather.2.cloned.1.call-done, bf16[2048,512]{1,0:T(8,128)(2,1)} %bitcast.48), kind=kOutput, calls=%fused_computation.29 | convolution fusion | flops 2421686272 | bytes 12845056 | tf_op jit(solution)/shard_map/dot_general | solution.py:90
  148.6 3.9 maximum_bitcast_fusion
  152.5 0.7 mul.111
  153.2 5.3 %all-to-all-start.1 = ((f32[64,1,32]{2,1,0:T(1,128)}), f32[64,1,32]{2,1,0:T(1,128)S(1)}, u32[]{:S(2)}, u32[]{:S(2)}) async-start(f32[64,1,32]{2,1,0:T(1,128)} %bitcast.10), calls=%async_computation.1 | async-start | bytes 65536 | tf_op jit(solution)/shard_map/all_to_all | solution.py:74
  158.6 9.5 %all-to-all-done.1 = f32[64,1,32]{2,1,0:T(1,128)S(1)} async-done(((f32[64,1,32]{2,1,0:T(1,128)}), f32[64,1,32]{2,1,0:T(1,128)S(1)}, u32[]{:S(2)}, u32[]{:S(2)}) %all-to-all-start.1) | async-done | bytes 8224 | tf_op jit(solution)/shard_map/all_to_all | solution.py:74
  168.0 0.5 broadcast.88
  168.6 0.7 reduce.3
  169.4 10.5 %gather_fusion.1 = f32[1024]{0:T(1024)} fusion(f32[2048]{0:T(1024)S(1)} %reshape.69, s32[1024]{0:T(1024)S(1)} %broadcast_clamp_fusion), kind=kCustom, calls=%fused_computation.1 | custom fusion | bytes 12288 | tf_op jit(solution)/shard_map/gather | solution.py:77
  179.9 139.0 %all-reduce.3.cloned.1.call-done = f32[256,256]{1,0:T(8,128)} async-done(((f32[256,256]{1,0:T(8,128)}), f32[256,256]{1,0:T(8,128)}) %all-reduce.3.cloned.1.call-update) | async-done | bytes 262160 | tf_op jit(solution)/shard_map/psum | solution.py:95
  319.0 49.5 %reduce-scatter.2.cloned.1.call-done = f32[1,2,256,512]{3,2,1,0:T(8,128)} async-done(((f32[1,2,256,2048]{3,2,1,0:T(8,128)}), f32[1,2,256,512]{3,2,1,0:T(8,128)}) %reduce-scatter.2.cloned.1.call-update) | async-done | bytes 1048592 | tf_op jit(solution)/shard_map/reduce_scatter | solution.py:97
  368.5 3.7 divide_subtract_fusion
  372.2 45.2 %all-reduce.5.cloned.1.call-done = f32[256,256]{1,0:T(8,128)} async-done(((f32[256,256]{1,0:T(8,128)}), f32[256,256]{1,0:T(8,128)}) %all-reduce.5.cloned.1.call-update) | async-done | bytes 262160 | tf_op jit(solution)/shard_map/psum | solution.py:95
  417.3 1.7 copy.26
  (38 shorter events, 0.6 us)
Async XLA Ops:
  7.2 20.9 %copy-start = (bf16[2048,256]{1,0:T(8,128)(2,1)S(1)}, bf16[2048,256]{1,0:T(8,128)(2,1)}, u32[]{:S(2)}) copy-start(bf16[2048,256]{1,0:T(8,128)(2,1)} %param.8) | copy-start | bytes 3145732
  7.2 20.8 %copy-start.8 = (s32[1024,1]{0,1:T(1,128)S(1)}, s32[1024,1]{0,1:T(1,128)}, u32[]{:S(2)}) copy-start(s32[1024,1]{0,1:T(1,128)} %param.10) | copy-start | bytes 12292
  28.1 4.2 copy-start.6
  38.9 63.5 %all-to-all-start = ((bf16[64,32,512]{2,1,0:T(8,128)(2,1)}), bf16[64,32,512]{2,1,0:T(8,128)(2,1)S(1)}, u32[]{:S(2)}, u32[]{:S(2)}) async-start(bf16[64,32,512]{2,1,0:T(8,128)(2,1)} %bitcast.6), calls=%async_computation | async-start | bytes 4194304 | tf_op jit(solution)/shard_map/all_to_all | solution.py:55
  51.0 51.4 %copy-start.7 = (bf16[256,256]{1,0:T(8,128)(2,1)S(1)}, bf16[256,256]{1,0:T(8,128)(2,1)}, u32[]{:S(2)}) copy-start(bf16[256,256]{1,0:T(8,128)(2,1)} %param.12) | copy-start | bytes 393220
  51.1 53.3 %all-gather.2.cloned.1.call-start = ((), (), s32[]{:S(2)}) async-start(), calls=%async_computation.3 | async-start | bytes 2621440 | tf_op jit(solution)/shard_map/all_gather | solution.py:50
  53.2 265.7 %all-reduce.3.cloned.1.call-start = ((), (), s32[]{:S(2)}) async-start(), calls=%async_computation.4 | async-start | bytes 524288 | tf_op jit(solution)/shard_map/psum | solution.py:95
  102.4 12.2 %copy-start.1 = (bf16[64,32,512]{2,1,0:T(8,128)(2,1)}, bf16[64,32,512]{2,1,0:T(8,128)(2,1)S(1)}, u32[]{:S(2)}) copy-start(bf16[64,32,512]{2,1,0:T(8,128)(2,1)S(1)} %all-to-all-done) | copy-start | bytes 6291460
  104.4 10.2 %copy-start.9 = (bf16[1,2,256,2048]{3,2,1,0:T(8,128)(2,1)S(1)}, bf16[1,2,256,2048]{3,2,1,0:T(8,128)(2,1)}, u32[]{:S(2)}) copy-start(bf16[1,2,256,2048]{3,2,1,0:T(8,128)(2,1)} %all-gather.2.cloned.1.call-done) | copy-start | bytes 6291460
  119.5 13.4 %copy-start.2 = (bf16[64,32,512]{2,1,0:T(8,128)(2,1)S(1)}, bf16[64,32,512]{2,1,0:T(8,128)(2,1)}, u32[]{:S(2)}) copy-start(bf16[64,32,512]{2,1,0:T(8,128)(2,1)} %copy-done.1) | copy-start | bytes 6291460
  119.5 13.3 %copy-start.4 = (f32[2048,256]{1,0:T(8,128)S(1)}, f32[2048,256]{1,0:T(8,128)}, u32[]{:S(2)}) copy-start(f32[2048,256]{1,0:T(8,128)} %fusion.12) | copy-start | bytes 6291460
  148.5 220.0 %reduce-scatter.2.cloned.1.call-start = ((), (), s32[]{:S(2)}) async-start(), calls=%async_computation.6 | async-start | bytes 5242880 | tf_op jit(solution)/shard_map/reduce_scatter | solution.py:97
  153.2 14.9 %all-to-all-start.1 = ((f32[64,1,32]{2,1,0:T(1,128)}), f32[64,1,32]{2,1,0:T(1,128)S(1)}, u32[]{:S(2)}, u32[]{:S(2)}) async-start(f32[64,1,32]{2,1,0:T(1,128)} %bitcast.10), calls=%async_computation.1 | async-start | bytes 65536 | tf_op jit(solution)/shard_map/all_to_all | solution.py:74
  158.5 258.8 %all-reduce.5.cloned.1.call-start = ((), (), s32[]{:S(2)}) async-start(), calls=%async_computation.5 | async-start | bytes 524288 | tf_op jit(solution)/shard_map/psum | solution.py:95
  169.4 199.1 %copy-start.3 = (f32[1,2,256,512]{3,2,1,0:T(8,128)S(1)}, f32[1,2,256,512]{3,2,1,0:T(8,128)}, u32[]{:S(2)}) copy-start(f32[1,2,256,512]{3,2,1,0:T(8,128)} %param.13) | copy-start | bytes 3145732
  169.4 199.1 %copy-start.5 = (f32[1,2,256,512]{3,2,1,0:T(8,128)S(1)}, f32[1,2,256,512]{3,2,1,0:T(8,128)}, u32[]{:S(2)}) copy-start(f32[1,2,256,512]{3,2,1,0:T(8,128)} %param.14) | copy-start | bytes 3145732
Sparse Core Ops, SparseCore 0:
  54.3 33.5 all-gather.1
  148.6 170.2 all-reduce.2
  321.7 46.7 reduce-scatter.1
  370.6 46.6 all-reduce.4
